TPU v7x, 256 devices: a whole 4x4x8 slice. The times are simulated.
256 devices in a mesh: freq: 16 (over z, core), tile: 16 (over y, x).
Axes of the slice: x: 4, y: 4, z: 8, core: 2. Of those that a mesh axis runs over, the one named last changes fastest.
Arguments:
- focal_field: bfloat16 [16, 16384, 2, 256], P('freq', 'tile'), may hold values from -6 to 6
- v_factors: bfloat16 [16, 16, 16384, 128], P('freq', None, 'tile'), may hold values from -0.1875 to 0.1875
- u_factors: bfloat16 [16, 16384, 16, 128], P('freq', 'tile'), may hold values from -0.125 to 0.125
- ranks: int32 [16, 16, 16], P('freq', None, 'tile'), may hold values from 16 to 64, as said below
- tile_mask: int32 [16, 16, 16], P('freq', None, 'tile'), may hold values 0 or 1
- initial_focus: bfloat16 [16, 32, 1024, 256], P('tile', None, 'freq'), may hold values from -6 to 6
- mute_starts: int32 [16, 1024, 256], P('tile', 'freq'), may hold values from 1 to 31
- taper: float32 [16, 1024], P('tile', 'freq'), may hold values from 0.3 to 3
Outputs:
- focusing: bfloat16 [16, 32, 1024, 256], P('tile', None, 'freq')
- correlation: float32 [16, 256, 256], P('freq', 'tile')
Inputs may be any that keep to these rules, and one draw needn't show every extreme that they name: `ranks`: in every frequency some tile has rank exactly 64; no rank is below 16.
All inputs are finite; a program needn't handle non-finite values. No bound on the sum of `tile_mask` on one device may be relied on, other than what follows from the above.
Results may differ from a plain program's by a relative error of at most 0.009.
Values may be sent and summed in bfloat16 or wider, within the bound.
No kernel may reach another device: no remote copies, remote signals or barrier semaphores. Data moves between devices by JAX's collectives and lax.ppermute only.
A program may use at most 64 MiB of HBM per device.

v0:
```python
import math
import jax
import jax.numpy as jnp
from jax import lax
from jax.sharding import PartitionSpec as P


def dft_table(trace_length, freq_count):
    clock_moments = jnp.arange(trace_length, dtype=jnp.float32)
    angular_rate = jnp.arange(freq_count, dtype=jnp.float32) + 1.0
    rotation_radians = 2.0 * math.pi / trace_length * clock_moments[:, None] * angular_rate[None, :]
    return jnp.stack([jnp.cos(rotation_radians), -jnp.sin(rotation_radians)], axis=2) / jnp.sqrt(
        jnp.float32(freq_count)
    )


def stacked_rhs(received):
    sources = received.shape[0]
    columns = received.shape[3]
    real_c = received[:, :, 0, :]
    imag_c = received[:, :, 1, :]
    upper = jnp.concatenate([real_c, -imag_c], axis=1)
    lower = jnp.concatenate([imag_c, real_c], axis=1)
    return jnp.concatenate([upper, lower], axis=2).reshape(sources * upper.shape[1], 2 * columns)


def body(focal_field, v_factors, u_factors, ranks, tile_mask, initial_focus, mute_starts, taper):
    tile_count = lax.axis_size("tile")
    rank_max = v_factors.shape[3] // 2
    focal_count = focal_field.shape[3]
    tile_rows = focal_field.shape[1]
    flat_field = focal_field[0].reshape(tile_rows, 2 * focal_count)
    moments = jnp.einsum(
        "irk,rc->ikc", v_factors[0], flat_field, preferred_element_type=jnp.float32
    )
    real_part = moments[:, :rank_max, :focal_count] - moments[:, rank_max:, focal_count:]
    imag_part = moments[:, :rank_max, focal_count:] + moments[:, rank_max:, :focal_count]
    levels = jnp.arange(rank_max, dtype=jnp.int32)
    retained = (
        (levels[None, :] < ranks[0, :, 0][:, None]) & (tile_mask[0, :, 0][:, None] > 0)
    ).astype(jnp.float32)
    coeffs = jnp.stack(
        [real_part * retained[:, :, None], imag_part * retained[:, :, None]], axis=2
    ).astype(jnp.bfloat16)
    u_rows = u_factors[0]
    received = lax.all_to_all(coeffs, "tile", split_axis=0, concat_axis=0, tiled=True)
    columns = received.shape[3]
    product = jnp.dot(
        u_rows.reshape(tile_rows, -1), stacked_rhs(received), preferred_element_type=jnp.float32
    )
    fields = product.reshape(tile_rows, 2, columns).astype(jnp.bfloat16)
    trace_length = initial_focus.shape[1]
    gathered = lax.all_to_all(fields[None], "freq", split_axis=1, concat_axis=0, tiled=True)
    dft_weights = dft_table(trace_length, gathered.shape[0])
    trace_signal = jnp.einsum(
        "tfc,fscn->tsn", dft_weights, gathered.astype(jnp.float32), precision=lax.Precision.HIGHEST
    )
    group_rows = trace_signal.shape[1]
    clock_moments = jnp.arange(trace_length, dtype=jnp.int32)
    silenced_wavefield = jnp.where(
        clock_moments[:, None, None] < mute_starts[0][None, :, :], trace_signal, 0.0
    )
    focusing = (initial_focus[0].astype(jnp.float32) - silenced_wavefield).astype(jnp.bfloat16)
    weighted = (focusing.astype(jnp.float32) * taper[0][None, :, None]).astype(jnp.bfloat16)
    flat_focus = focusing.reshape(trace_length * group_rows, focal_count)
    flat_weighted = weighted.reshape(trace_length * group_rows, focal_count)
    partial_value = lax.dot_general(
        flat_focus, flat_weighted, (((0,), (0,)), ((), ())), preferred_element_type=jnp.float32
    )
    normalizer = 1.0 / float(tile_count * trace_length * group_rows)
    summed_total = lax.psum(partial_value.astype(jnp.bfloat16), "tile").astype(jnp.float32)
    share_rows = focal_count // tile_count
    own_rows = lax.dynamic_slice_in_dim(
        summed_total, lax.axis_index("tile") * share_rows, share_rows, 0
    )
    return (focusing[None], (own_rows * normalizer)[None])


def solution(mesh):
    placed = (
        P("freq", "tile", None, None),
        P("freq", None, "tile", None),
        P("freq", "tile", None, None),
        P("freq", None, "tile"),
        P("freq", None, "tile"),
        P("tile", None, "freq", None),
        P("tile", "freq", None),
        P("tile", "freq"),
    )
    return jax.shard_map(
        body,
        mesh=mesh,
        in_specs=placed,
        out_specs=(P("tile", None, "freq", None), P("freq", "tile", None)),
        check_vma=False,
    )
```

profile of v0, /device:TPU:2, one launch (start us, length us, event | category | flops | bytes accessed | tf_op | source)
XLA Modules:
  0.0 179.9 jit_solution(2746314441526483126)
XLA Ops:
  7.2 0.0 copy-start.5
  7.2 1.7 reshape.179
  8.9 0.0 copy-done.5
  8.9 0.0 copy-start.1
  9.0 4.6 %fusion.3 = f32[16,128,512]{2,1,0:T(8,128)S(1)} fusion(bf16[1024,512,1]{1,0,2:T(8,128)(2,1)S(1)} %reshape.179, bf16[1,16,1024,128]{3,2,1,0:T(8,128)(2,1)} %param.9), kind=kOutput, calls=%fused_computation.3 | convolution fusion | flops 2147483648 | bytes 9437184 | tf_op jit(solution)/shard_map/irk,rc->ikc/dot_general | solution.py:33
  13.5 0.0 copy-done.1
  13.6 0.1 fusion.27
  13.6 0.4 fusion.18
  14.0 0.1 pad_maximum_fusion
  14.1 0.1 copy.24
  14.2 23.1 %all_to_all.17 = bf16[16,64,2,256]{3,1,2,0:T(8,128)(2,1)S(1)} all-to-all(bf16[16,64,2,256]{3,1,2,0:T(8,128)(2,1)S(1)} %copy.24), channel_id=1, replica_groups=mesh['freq'=16,'tile'=16] {'tile'}, dimensions={0} | all-to-all | bytes 2097152 | tf_op jit(solution)/shard_map/all_to_all | solution.py:46
  37.3 0.1 slice_bitcast_fusion
  37.4 0.0 copy-start.2
  37.4 0.2 maximum_maximum_fusion
  37.6 1.9 %copy-done.2 = bf16[1,1024,16,128]{3,2,1,0:T(8,128)(2,1)S(1)} copy-done((bf16[1,1024,16,128]{3,2,1,0:T(8,128)(2,1)S(1)}, bf16[1,1024,16,128]{3,2,1,0:T(8,128)(2,1)}, u32[]{:S(2)}) %copy-start.2) | copy-done | bytes 4194328
  39.6 2.4 %fusion.7 = bf16[512,1024]{1,0:T(8,128)(2,1)S(1)} fusion(bf16[2048,512]{1,0:T(8,128)(2,1)S(1)} %bitcast.54, bf16[128,8,16,128]{3,2,1,0:T(8,128)(2,1)S(1)} %bitcast.59), kind=kOutput, calls=%fused_computation.12 | convolution fusion | flops 2148007936 | bytes 7340032 | tf_op jit(solution)/shard_map/dot_general | solution.py:48
  42.0 0.0 copy-start.3
  42.0 0.0 copy-start.4
  42.0 2.0 %copy.26 = bf16[1,1024,2,256]{3,2,0,1:T(2,128)(2,1)} copy(bf16[1,1024,2,256]{1,3,2,0:T(8,128)(2,1)S(1)} %bitcast.56) | data formatting | bytes 2097152 | tf_op jit(solution)/shard_map/convert_element_type | solution.py:51
  44.0 8.6 %all-to-all-start.1 = ((bf16[1,1024,2,256]{3,2,0,1:T(2,128)(2,1)}), bf16[1,1024,2,256]{3,2,0,1:T(2,128)(2,1)S(1)}, u32[]{:S(2)}, u32[]{:S(2)}) async-start(bf16[1,1024,2,256]{3,2,0,1:T(2,128)(2,1)} %copy.26), calls=%async_computation.1 | async-start | bytes 2097152 | tf_op jit(solution)/shard_map/all_to_all | solution.py:53
  52.6 0.0 copy-start
  52.6 0.0 all-reduce.2.cloned.1.call-start
  52.7 0.1 multiply_cosine_fusion
  52.8 26.3 %all-to-all-done.1 = bf16[1,1024,2,256]{3,2,0,1:T(2,128)(2,1)S(1)} async-done(((bf16[1,1024,2,256]{3,2,0,1:T(2,128)(2,1)}), bf16[1,1024,2,256]{3,2,0,1:T(2,128)(2,1)S(1)}, u32[]{:S(2)}, u32[]{:S(2)}) %all-to-all-start.1) | async-done | bytes 1048608 | tf_op jit(solution)/shard_map/all_to_all | solution.py:53
  79.1 0.0 copy-done.3
  79.1 0.0 copy-done.4
  79.1 1.9 %fusion.5 = bf16[32,64,256]{2,0,1:T(8,128)(2,1)S(1)} fusion(bf16[16,64,2,256]{3,2,1,0:T(2,128)(2,1)S(1)} %bitcast.55, bf16[1,32,64,256]{3,2,1,0:T(8,128)(2,1)S(1)} %copy-done.3, s32[64,256]{1,0:T(8,128)S(1)} %bitcast.60, f32[32,16,1]{0,1,2:T(8,128)S(1)} %get-tuple-element.13, f32[32,16,1]{0,1,2:T(8,128)S(1)} %get-tuple-element.12), kind=kOutput, calls=%fused_computation.7 | convolution fusion | flops 203950080 | bytes 3215360 | tf_op jit(solution)/shard_map/tfc,fscn->tsn/dot_general | solution.py:55
  81.0 0.0 copy-done
  81.1 1.3 fusion.11
  82.4 0.0 all-reduce.2.cloned.1.call-update
  82.4 1.6 copy.29
  83.9 87.8 %all-reduce.2.cloned.1.call-done = bf16[256,256]{1,0:T(8,128)(2,1)} async-done(((bf16[256,256]{1,0:T(8,128)(2,1)}), bf16[256,256]{1,0:T(8,128)(2,1)}) %all-reduce.2.cloned.1.call-update) | async-done | bytes 131088 | tf_op jit(solution)/shard_map/psum | solution.py:71
  171.7 1.3 multiply_bitcast_fusion
  (4 shorter events, 0.1 us)
Async XLA Ops:
  7.2 1.8 copy-start.5
  8.9 4.6 %copy-start.1 = (s32[1,16,1]{1,2,0:T(1,128)S(1)}, s32[1,16,1]{1,2,0:T(1,128)}, u32[]{:S(2)}) copy-start(s32[1,16,1]{1,2,0:T(1,128)} %param.11) | copy-start | bytes 196
  37.4 2.2 %copy-start.2 = (bf16[1,1024,16,128]{3,2,1,0:T(8,128)(2,1)S(1)}, bf16[1,1024,16,128]{3,2,1,0:T(8,128)(2,1)}, u32[]{:S(2)}) copy-start(bf16[1,1024,16,128]{3,2,1,0:T(8,128)(2,1)} %param.10) | copy-start | bytes 12582916
  42.0 37.1 %copy-start.3 = (bf16[1,32,64,256]{3,2,1,0:T(8,128)(2,1)S(1)}, bf16[1,32,64,256]{3,2,1,0:T(8,128)(2,1)}, u32[]{:S(2)}) copy-start(bf16[1,32,64,256]{3,2,1,0:T(8,128)(2,1)} %param.13) | copy-start | bytes 3145732
  42.0 37.1 %copy-start.4 = (s32[1,64,256]{2,1,0:T(8,128)S(1)}, s32[1,64,256]{2,1,0:T(8,128)}, u32[]{:S(2)}) copy-start(s32[1,64,256]{2,1,0:T(8,128)} %param.14) | copy-start | bytes 196612
  44.0 35.1 %all-to-all-start.1 = ((bf16[1,1024,2,256]{3,2,0,1:T(2,128)(2,1)}), bf16[1,1024,2,256]{3,2,0,1:T(2,128)(2,1)S(1)}, u32[]{:S(2)}, u32[]{:S(2)}) async-start(bf16[1,1024,2,256]{3,2,0,1:T(2,128)(2,1)} %copy.26), calls=%async_computation.1 | async-start | bytes 2097152 | tf_op jit(solution)/shard_map/all_to_all | solution.py:53
  52.6 28.4 %copy-start = (f32[1,64]{1,0:T(1,128)S(1)}, f32[1,64]{1,0:T(1,128)}, u32[]{:S(2)}) copy-start(f32[1,64]{1,0:T(1,128)} %param.15) | copy-start | bytes 772
  52.6 119.1 %all-reduce.2.cloned.1.call-start = ((), (), s32[]{:S(2)}) async-start(), calls=%async_computation.2 | async-start | bytes 262144 | tf_op jit(solution)/shard_map/psum | solution.py:71
Sparse Core Ops, SparseCore 0:
  82.5 89.1 all-reduce.1
where the time goes:
time: 180 us
  waiting for transfers between devices  114 us (63%)
  blocking collectives  23.1 us (13%)
  between operations  14.2 us (8%)
  matrix products  10.2 us (6%)
  starting transfers between devices  8.61 us (5%)
  local copies, waits for them, and re-layouts  7.51 us (4%)
  other arithmetic  2.2 us (1%)
    psum x1, waiting for transfers between devices, body(): lax.psum(partial_value.astype(jnp.bfloat16), 'tile').astype(jnp.float32)  87.8 us
    all_to_all x1, waiting for transfers between devices, body(): lax.all_to_all(fields[None], 'freq', split_axis=1, concat_axis=0, tiled=T...  26.3 us
    all_to_all x1, blocking collectives, body(): lax.all_to_all(coeffs, 'tile', split_axis=0, concat_axis=0, tiled=True)  23.1 us
    all_to_all x1, starting transfers between devices, body(): lax.all_to_all(fields[None], 'freq', split_axis=1, concat_axis=0, tiled=T...  8.57 us
    dot_general x1, matrix products, body(): jnp.einsum('irk,rc->ikc', v_factors[0], flat_field, preferred_element_typ...  4.58 us
  transfers between devices with their start and end apart: 2, of which 2 were waited for; matrix products, arithmetic and copies ran while one was open for 1% of the time, Pallas kernels for 0%

commit v1 on v0

--- a/solution.py
+++ b/solution.py
@@ -68,7 +68,9 @@
         flat_focus, flat_weighted, (((0,), (0,)), ((), ())), preferred_element_type=jnp.float32
     )
     normalizer = 1.0 / float(tile_count * trace_length * group_rows)
-    summed_total = lax.psum(partial_value.astype(jnp.bfloat16), "tile").astype(jnp.float32)
+    summed_total = jnp.sum(
+        jax.lax.all_gather(partial_value.astype(jnp.bfloat16), axis_name="tile"), 0
+    ).astype(jnp.float32)
     share_rows = focal_count // tile_count
     own_rows = lax.dynamic_slice_in_dim(
         summed_total, lax.axis_index("tile") * share_rows, share_rows, 0

time: 180 us -> 138 us (0.77)
  waiting for transfers between devices: 114 us -> 70.8 us
    psum x1 -> x0, waiting for transfers between devices: 87.8 us -> none  [body(): lax.psum(partial_value.astype(jnp.bfloat16), 'tile').astype(jnp.float32)]
    all_gather x0 -> x1, waiting for transfers between devices: none -> 44.5 us  [body(): jax.lax.all_gather(partial_value.astype(jnp.bfloat16), axis_name='tile')]
    reduce_sum x0 -> x1, other arithmetic: none -> 1.88 us  [body(): jnp.sum(jax.lax.all_gather(partial_value.astype(jnp.bfloat16), axis_name=...]
where the time goes in v1:
time: 138 us
  waiting for transfers between devices  70.8 us (51%)
  blocking collectives  23.1 us (17%)
  between operations  14.2 us (10%)
  matrix products  10.2 us (7%)
  starting transfers between devices  8.61 us (6%)
  local copies, waits for them, and re-layouts  7.48 us (5%)
  other arithmetic  3.4 us (2%)
    all_gather x1, waiting for transfers between devices, body(): jax.lax.all_gather(partial_value.astype(jnp.bfloat16), axis_name='tile')  44.5 us
    all_to_all x1, waiting for transfers between devices, body(): lax.all_to_all(fields[None], 'freq', split_axis=1, concat_axis=0, tiled=T...  26.3 us
    all_to_all x1, blocking collectives, body(): lax.all_to_all(coeffs, 'tile', split_axis=0, concat_axis=0, tiled=True)  23.1 us
    all_to_all x1, starting transfers between devices, body(): lax.all_to_all(fields[None], 'freq', split_axis=1, concat_axis=0, tiled=T...  8.57 us
    dot_general x1, matrix products, body(): jnp.einsum('irk,rc->ikc', v_factors[0], flat_field, preferred_element_typ...  4.58 us
    unnamed x13, local copies, waits for them, and re-layouts  3.53 us
  transfers between devices with their start and end apart: 2, of which 2 were waited for; matrix products, arithmetic and copies ran while one was open for 1% of the time, Pallas kernels for 0%

profile of v1, /device:TPU:2, one launch (start us, length us, event | category | flops | bytes accessed | tf_op | source)
XLA Modules:
  0.0 137.8 jit_solution(13781497539528874671)
XLA Ops:
  7.2 0.0 copy-start.5
  7.2 1.7 %reshape.180 = bf16[1024,512,1]{1,0,2:T(8,128)(2,1)S(1)} reshape(bf16[1,1024,2,256]{3,2,1,0:T(2,128)(2,1)} %param.8) | data formatting | bytes 2097152 | tf_op jit(solution)/shard_map/reshape;squeeze | solution.py:32
  8.9 0.0 copy-done.5
  8.9 0.0 copy-start.1
  9.0 4.6 %fusion.3 = f32[16,128,512]{2,1,0:T(8,128)S(1)} fusion(bf16[1024,512,1]{1,0,2:T(8,128)(2,1)S(1)} %reshape.180, bf16[1,16,1024,128]{3,2,1,0:T(8,128)(2,1)} %param.9), kind=kOutput, calls=%fused_computation.3 | convolution fusion | flops 2147483648 | bytes 9437184 | tf_op jit(solution)/shard_map/irk,rc->ikc/dot_general | solution.py:33
  13.5 0.0 copy-done.1
  13.6 0.1 fusion.27
  13.6 0.4 fusion.18
  14.0 0.1 pad_maximum_fusion
  14.1 0.1 copy.24
  14.2 23.1 %all_to_all.17 = bf16[16,64,2,256]{3,1,2,0:T(8,128)(2,1)S(1)} all-to-all(bf16[16,64,2,256]{3,1,2,0:T(8,128)(2,1)S(1)} %copy.24), channel_id=1, replica_groups=mesh['freq'=16,'tile'=16] {'tile'}, dimensions={0} | all-to-all | bytes 2097152 | tf_op jit(solution)/shard_map/all_to_all | solution.py:46
  37.3 0.1 slice_bitcast_fusion
  37.4 0.0 copy-start.2
  37.4 0.2 maximum_maximum_fusion
  37.6 1.9 %copy-done.2 = bf16[1,1024,16,128]{3,2,1,0:T(8,128)(2,1)S(1)} copy-done((bf16[1,1024,16,128]{3,2,1,0:T(8,128)(2,1)S(1)}, bf16[1,1024,16,128]{3,2,1,0:T(8,128)(2,1)}, u32[]{:S(2)}) %copy-start.2) | copy-done | bytes 4194328
  39.5 2.4 %fusion.7 = bf16[512,1024]{1,0:T(8,128)(2,1)S(1)} fusion(bf16[2048,512]{1,0:T(8,128)(2,1)S(1)} %bitcast.55, bf16[128,8,16,128]{3,2,1,0:T(8,128)(2,1)S(1)} %bitcast.61), kind=kOutput, calls=%fused_computation.12 | convolution fusion | flops 2148007936 | bytes 7340032 | tf_op jit(solution)/shard_map/dot_general | solution.py:48
  41.9 0.0 copy-start.3
  42.0 0.0 copy-start.4
  42.0 2.0 %copy.26 = bf16[1,1024,2,256]{3,2,0,1:T(2,128)(2,1)} copy(bf16[1,1024,2,256]{1,3,2,0:T(8,128)(2,1)S(1)} %bitcast.58) | data formatting | bytes 2097152 | tf_op jit(solution)/shard_map/convert_element_type | solution.py:51
  44.0 8.6 %all-to-all-start.1 = ((bf16[1,1024,2,256]{3,2,0,1:T(2,128)(2,1)}), bf16[1,1024,2,256]{3,2,0,1:T(2,128)(2,1)S(1)}, u32[]{:S(2)}, u32[]{:S(2)}) async-start(bf16[1,1024,2,256]{3,2,0,1:T(2,128)(2,1)} %copy.26), calls=%async_computation.1 | async-start | bytes 2097152 | tf_op jit(solution)/shard_map/all_to_all | solution.py:53
  52.6 0.0 copy-start
  52.6 0.0 all-gather.3.cloned.1.call-start
  52.7 0.1 multiply_cosine_fusion
  52.8 26.3 %all-to-all-done.1 = bf16[1,1024,2,256]{3,2,0,1:T(2,128)(2,1)S(1)} async-done(((bf16[1,1024,2,256]{3,2,0,1:T(2,128)(2,1)}), bf16[1,1024,2,256]{3,2,0,1:T(2,128)(2,1)S(1)}, u32[]{:S(2)}, u32[]{:S(2)}) %all-to-all-start.1) | async-done | bytes 1048608 | tf_op jit(solution)/shard_map/all_to_all | solution.py:53
  79.1 0.0 copy-done.3
  79.1 0.0 copy-done.4
  79.1 1.9 %fusion.5 = bf16[32,64,256]{2,0,1:T(8,128)(2,1)S(1)} fusion(bf16[16,64,2,256]{3,2,1,0:T(2,128)(2,1)S(1)} %bitcast.57, bf16[1,32,64,256]{3,2,1,0:T(8,128)(2,1)S(1)} %copy-done.3, s32[64,256]{1,0:T(8,128)S(1)} %bitcast.62, f32[32,16,1]{0,1,2:T(8,128)S(1)} %get-tuple-element.13, f32[32,16,1]{0,1,2:T(8,128)S(1)} %get-tuple-element.12), kind=kOutput, calls=%fused_computation.7 | convolution fusion | flops 203950080 | bytes 3215360 | tf_op jit(solution)/shard_map/tfc,fscn->tsn/dot_general | solution.py:55
  81.0 0.0 copy-done
  81.0 1.3 fusion.11
  82.3 0.0 all-gather.3.cloned.1.call-update
  82.3 1.6 %copy.29 = bf16[1,32,64,256]{3,2,1,0:T(8,128)(2,1)} copy(bf16[1,32,64,256]{3,1,2,0:T(8,128)(2,1)S(1)} %bitcast.54) | data formatting | bytes 2097152
  83.9 44.5 %all-gather.3.cloned.1.call-done = bf16[4096,256]{1,0:T(8,128)(2,1)} async-done(((bf16[256,256]{1,0:T(8,128)(2,1)}), bf16[4096,256]{1,0:T(8,128)(2,1)}) %all-gather.3.cloned.1.call-update) | async-done | bytes 2097168 | tf_op jit(solution)/shard_map/all_gather | solution.py:72
  128.4 1.9 %reduce_sum.12 = bf16[256,256]{1,0:T(8,128)(2,1)S(1)} reduce(bf16[16,256,256]{2,1,0:T(8,128)(2,1)} %bitcast.56, bf16[]{:T(256)} %constant.7.clone.1), dimensions={0}, to_apply=%region_0.1 | reduce | flops 983040 | bytes 2228226 | tf_op jit(solution)/shard_map/reduce_sum | solution.py:71
  130.3 0.6 multiply_bitcast_fusion
  (4 shorter events, 0.1 us)
Async XLA Ops:
  7.2 1.8 %copy-start.5 = (s32[1,16,1]{1,2,0:T(1,128)S(1)}, s32[1,16,1]{1,2,0:T(1,128)}, u32[]{:S(2)}) copy-start(s32[1,16,1]{1,2,0:T(1,128)} %param.12) | copy-start | bytes 196
  8.9 4.6 %copy-start.1 = (s32[1,16,1]{1,2,0:T(1,128)S(1)}, s32[1,16,1]{1,2,0:T(1,128)}, u32[]{:S(2)}) copy-start(s32[1,16,1]{1,2,0:T(1,128)} %param.11) | copy-start | bytes 196
  37.4 2.2 %copy-start.2 = (bf16[1,1024,16,128]{3,2,1,0:T(8,128)(2,1)S(1)}, bf16[1,1024,16,128]{3,2,1,0:T(8,128)(2,1)}, u32[]{:S(2)}) copy-start(bf16[1,1024,16,128]{3,2,1,0:T(8,128)(2,1)} %param.10) | copy-start | bytes 12582916
  41.9 37.1 %copy-start.3 = (bf16[1,32,64,256]{3,2,1,0:T(8,128)(2,1)S(1)}, bf16[1,32,64,256]{3,2,1,0:T(8,128)(2,1)}, u32[]{:S(2)}) copy-start(bf16[1,32,64,256]{3,2,1,0:T(8,128)(2,1)} %param.13) | copy-start | bytes 3145732
  42.0 37.1 %copy-start.4 = (s32[1,64,256]{2,1,0:T(8,128)S(1)}, s32[1,64,256]{2,1,0:T(8,128)}, u32[]{:S(2)}) copy-start(s32[1,64,256]{2,1,0:T(8,128)} %param.14) | copy-start | bytes 196612
  44.0 35.1 %all-to-all-start.1 = ((bf16[1,1024,2,256]{3,2,0,1:T(2,128)(2,1)}), bf16[1,1024,2,256]{3,2,0,1:T(2,128)(2,1)S(1)}, u32[]{:S(2)}, u32[]{:S(2)}) async-start(bf16[1,1024,2,256]{3,2,0,1:T(2,128)(2,1)} %copy.26), calls=%async_computation.1 | async-start | bytes 2097152 | tf_op jit(solution)/shard_map/all_to_all | solution.py:53
  52.6 28.4 %copy-start = (f32[1,64]{1,0:T(1,128)S(1)}, f32[1,64]{1,0:T(1,128)}, u32[]{:S(2)}) copy-start(f32[1,64]{1,0:T(1,128)} %param.15) | copy-start | bytes 772
  52.6 75.9 %all-gather.3.cloned.1.call-start = ((), (), s32[]{:S(2)}) async-start(), calls=%async_computation.2 | async-start | bytes 2228224 | tf_op jit(solution)/shard_map/all_gather | solution.py:72
Sparse Core Ops, SparseCore 0:
  82.5 45.9 all-gather.2
